TPU v7x, 512 devices: a whole 4x4x16 slice. The times are simulated.
512 devices in a mesh: rows: 128 (over y, x, z_lo), rep: 4 (over z_hi, core).
Axes of the slice: x: 4, y: 4, z: 16 (z_hi: 2, z_lo: 8; z = z_hi * 8 + z_lo), core: 2. Of those that a mesh axis runs over, the one named last changes fastest.
Arguments:
- covariates: bfloat16 [1048576, 128], P(('rows', 'rep')), may hold values from -6 to 6
- treated: int32 [1048576], P(('rows', 'rep')), may hold values 0 or 1
- landmarks: bfloat16 [1024, 128], P('rows'), may hold values from -6 to 6
- land_treat: bfloat16 [1024], P('rows'), may hold values from 0 to 1
Outputs:
- gram: float32 [1024, 512], P('rows')
- moment: float32 [1024], P('rows')
All inputs are finite; a program needn't handle non-finite values. No bound on the sum of `treated` on one device may be relied on, other than what follows from the above.
Results may differ from a plain program's by a relative error of at most 0.0034.
Values may be sent and summed in bfloat16 or wider, within the bound.
No kernel may reach another device: no remote copies, remote signals or barrier semaphores. Data moves between devices by JAX's collectives and lax.ppermute only.
A program may use at most 64 MiB of HBM per device.

v0:
```python
import jax
import jax.numpy as jnp
from jax import lax
from jax.sharding import PartitionSpec as P

PANELS = 2
gamma_rate = 0.03125


def on_device(covariates, treated, landmarks, land_treat):
    width = covariates.shape[1]
    total_rows = covariates.shape[0] * lax.axis_size("rows") * lax.axis_size("rep")
    all_land, all_treat = (
        lax.all_gather(landmarks, "rows", axis=0, tiled=True),
        lax.all_gather(land_treat, "rows", axis=0, tiled=True),
    )
    rows_f = covariates.astype(jnp.float32)
    sq_rows = jnp.sum(rows_f * rows_f, axis=1)[:, None]
    land_f = all_land.astype(jnp.float32)
    sq_land = jnp.sum(land_f * land_f, axis=1)
    lt_value = all_treat.astype(jnp.float32)
    on_one = jnp.exp(-0.5 * jnp.square(1.0 - lt_value))
    on_zero = jnp.exp(-0.5 * jnp.square(lt_value))
    is_treated = treated[:, None] == 1
    panel_size = all_land.shape[0] // PANELS
    gram_terms = []
    kern_terms = []
    for panel in range(PANELS):
        first = panel * panel_size
        block = all_land[first : first + panel_size]
        cross = lax.dot_general(
            covariates, block, (((1,), (1,)), ((), ())), preferred_element_type=jnp.float32
        )
        kern = jnp.exp(
            gamma_rate
            * (2.0 * width - sq_rows - sq_land[None, first : first + panel_size] + 2.0 * cross)
        )
        factor = jnp.where(
            is_treated,
            on_one[None, first : first + panel_size],
            on_zero[None, first : first + panel_size],
        )
        features = (kern * factor).astype(jnp.bfloat16)
        gram_part = lax.dot_general(
            features, features, (((0,), (0,)), ((), ())), preferred_element_type=jnp.float32
        )
        gram_terms.append(gram_part / total_rows)
        kern_terms.append(jnp.sum(kern, axis=0) / total_rows)
    gram_term = jnp.concatenate(gram_terms, axis=0)
    moment_term = (on_one - on_zero) * jnp.concatenate(kern_terms, axis=0)
    shares = (
        lax.psum_scatter(gram_term, "rows", scatter_dimension=0, tiled=True),
        lax.psum_scatter(moment_term, "rows", scatter_dimension=0, tiled=True),
    )
    gram_out, moment_out = lax.psum((shares[0], shares[1]), "rep")
    return (gram_out, moment_out)


def solution(mesh):
    in_specs = (P(("rows", "rep"), None), P(("rows", "rep")), P("rows", None), P("rows"))
    out_specs = (P("rows", None), P("rows"))
    return jax.shard_map(
        on_device, mesh=mesh, in_specs=in_specs, out_specs=out_specs, check_vma=False
    )
```

profile of v0, /device:TPU:1, one launch (start us, length us, event | category | flops | bytes accessed | tf_op | source)
XLA Modules:
  0.0 2144.9 jit_solution(338041234744841244)
XLA Ops:
  7.2 0.0 copy-start
  7.2 0.0 reduce-scatter.2.cloned.1.call-start
  7.2 0.7 broadcast_compare_fusion
  8.0 1.3 fusion.20
  10.0 0.8 dynamic-update-slice
  10.8 477.4 %all-reduce = bf16[1024]{0:T(1024)(128)(2,1)S(1)} all-reduce(bf16[1024]{0:T(1024)(128)(2,1)S(1)} %dynamic-update-slice), channel_id=1, replica_groups=mesh['rows'=128,'rep'=4] {'rows'}, use_global_device_ids=true, to_apply=%add | all-reduce | flops 1024 | bytes 4096
  488.3 1.4 multiply_reduce_fusion
  489.7 457.1 %all_gather.6 = bf16[1024,128]{1,0:T(8,128)(2,1)S(1)} all-gather(bf16[8,128]{1,0:T(8,128)(2,1)} %param.6), channel_id=1, replica_groups=mesh['rows'=128,'rep'=4] {'rows'}, dimensions={0}, use_global_device_ids=true | all-gather | bytes 264192 | tf_op jit(solution)/shard_map/all_gather | solution.py:14
  946.7 0.2 multiply_reduce_fusion.1
  947.0 2.2 fusion.22
  949.2 0.0 copy-done
  949.2 1.1 fusion.21
  950.4 2.0 fusion.8
  952.3 2.0 fusion.9
  954.3 1.5 pad_maximum_fusion
  955.9 0.0 reduce-scatter.2.cloned.1.call-update
  956.5 463.3 %all-reduce.1 = f32[1024]{0:T(1024)S(1)} all-reduce(f32[1024]{0:T(1024)S(1)} %get-tuple-element.12), channel_id=3, replica_groups=mesh['rows'=128,'rep'=4] {'rows'}, use_global_device_ids=true, to_apply=%region_6.7.clone | all-reduce | flops 1024 | bytes 8192
  1419.8 0.1 dynamic-slice.2
  1419.9 584.4 %reduce-scatter.2.cloned.1.call-done = f32[8,512]{1,0:T(8,128)} async-done(((f32[1024,512]{1,0:T(8,128)}), f32[8,512]{1,0:T(8,128)}) %reduce-scatter.2.cloned.1.call-update) | async-done | bytes 16400 | tf_op jit(solution)/shard_map/reduce_scatter | solution.py:52
  2004.3 133.8 %all-reduce.2 = (f32[8,512]{1,0:T(8,128)}, f32[8]{0:T(128)}) all-reduce(f32[8,512]{1,0:T(8,128)} %reduce-scatter.2.cloned.1.call-done, f32[8]{0:T(128)S(1)} %dynamic-slice.2), channel_id=1, replica_groups=mesh['rows'=128,'rep'=4] {'rep'}, use_global_device_ids=true, to_apply=%region_3.4 | all-reduce | flops 4104 | bytes 32832 | tf_op jit(solution)/shard_map/psum | solution.py:55
  (7 shorter events, 0.0 us)
Async XLA Ops:
  7.2 942.0 %copy-start = (bf16[2048,128]{1,0:T(8,128)(2,1)S(1)}, bf16[2048,128]{1,0:T(8,128)(2,1)}, u32[]{:S(2)}) copy-start(bf16[2048,128]{1,0:T(8,128)(2,1)} %param.4) | copy-start | bytes 1572868
  7.2 1997.1 %reduce-scatter.2.cloned.1.call-start = ((), (), s32[]{:S(2)}) async-start(), calls=%async_computation.1 | async-start | bytes 2113536 | tf_op jit(solution)/shard_map/reduce_scatter | solution.py:52
Sparse Core Ops, SparseCore 0:
  956.0 1048.2 reduce-scatter.1
where the time goes:
time: 2150 us; the launch traced here: 2140 us
  blocking collectives  1530 us (71%)
  waiting for transfers between devices  584 us (27%)
    unnamed x2, blocking collectives  941 us
    reduce_scatter x1, waiting for transfers between devices, on_device(): lax.psum_scatter(gram_term, 'rows', scatter_dimension=0, tiled=True)  584 us
    all_gather x1, blocking collectives, on_device(): lax.all_gather(landmarks, 'rows', axis=0, tiled=True)  457 us
    psum x1, blocking collectives, on_device(): gram_out, moment_out = lax.psum((shares[0], shares[1]), 'rep')  134 us
  transfers between devices with their start and end apart: 1, of which 1 were waited for; matrix products, arithmetic and copies ran while one was open for 0% of the time, Pallas kernels for 0%

commit v1 on v0

--- a/solution.py
+++ b/solution.py
@@ -11,7 +11,9 @@
     width = covariates.shape[1]
     total_rows = covariates.shape[0] * lax.axis_size("rows") * lax.axis_size("rep")
     all_land, all_treat = (
-        lax.all_gather(landmarks, "rows", axis=0, tiled=True),
+        jnp.concatenate(
+            lax.all_to_all(jnp.stack([landmarks] * lax.axis_size("rows")), "rows", 0, 0), axis=0
+        ),
         lax.all_gather(land_treat, "rows", axis=0, tiled=True),
     )
     rows_f = covariates.astype(jnp.float32)

time: 2150 us -> 1650 us (0.77)
  blocking collectives: 1530 us -> 1070 us
  waiting for transfers between devices: 584 us -> 528 us
    all_gather x1 -> x0, blocking collectives: 457 us -> none  [on_device(): lax.all_gather(landmarks, 'rows', axis=0, tiled=True)]
    reduce_scatter x1, waiting for transfers between devices: 584 us -> 528 us  [on_device(): lax.psum_scatter(gram_term, 'rows', scatter_dimension=0, tiled=True)]
  transfers between devices with their start and end apart: 1 -> 2, of which waited for: 1 -> 1; matrix products, arithmetic and copies ran while one was open for 0% -> 0% of each run, Pallas kernels for 0% -> 0%
where the time goes in v1:
time: 1650 us
  blocking collectives  1070 us (65%)
  waiting for transfers between devices  528 us (32%)
  starting transfers between devices  20.4 us (1%)
    unnamed x2, blocking collectives  936 us
    reduce_scatter x1, waiting for transfers between devices, on_device(): lax.psum_scatter(gram_term, 'rows', scatter_dimension=0, tiled=True)  528 us
    psum x1, blocking collectives, on_device(): gram_out, moment_out = lax.psum((shares[0], shares[1]), 'rep')  137 us
  transfers between devices with their start and end apart: 2, of which 1 were waited for; matrix products, arithmetic and copies ran while one was open for 0% of the time, Pallas kernels for 0%

profile of v1, /device:TPU:1, one launch (start us, length us, event | category | flops | bytes accessed | tf_op | source)
XLA Modules:
  0.0 1651.5 jit_solution(7145002999546787419)
XLA Ops:
  7.2 0.0 copy-start
  7.2 1.5 stack.2
  8.6 20.4 %all-to-all-start = ((bf16[128,8,128]{2,1,0:T(8,128)(2,1)}), bf16[128,8,128]{2,1,0:T(8,128)(2,1)S(1)}, u32[]{:S(2)}, u32[]{:S(2)}) async-start(bf16[128,8,128]{2,1,0:T(8,128)(2,1)} %stack.2), calls=%async_computation | async-start | bytes 524288 | tf_op jit(solution)/shard_map/all_to_all | solution.py:15
  29.0 0.0 reduce-scatter.2.cloned.1.call-start
  29.1 1.4 fusion.18
  31.1 0.8 dynamic-update-slice
  32.0 473.0 %all-reduce = bf16[1024]{0:T(1024)(128)(2,1)S(1)} all-reduce(bf16[1024]{0:T(1024)(128)(2,1)S(1)} %dynamic-update-slice), channel_id=1, replica_groups=mesh['rows'=128,'rep'=4] {'rows'}, use_global_device_ids=true, to_apply=%add | all-reduce | flops 1024 | bytes 4096
  504.9 1.4 multiply_reduce_fusion
  506.3 0.7 broadcast_compare_fusion
  507.0 0.0 all-to-all-done
  507.0 0.2 multiply_reduce_fusion.1
  507.3 0.1 sub.48
  507.4 0.1 sub.53
  507.4 2.2 fusion.19
  509.6 0.0 copy-done
  509.6 1.1 fusion.20
  510.8 2.0 fusion.8
  512.8 2.0 fusion.9
  514.8 1.5 pad_maximum_fusion
  516.3 0.0 reduce-scatter.2.cloned.1.call-update
  517.0 463.4 %all-reduce.1 = f32[1024]{0:T(1024)S(1)} all-reduce(f32[1024]{0:T(1024)S(1)} %get-tuple-element.12), channel_id=3, replica_groups=mesh['rows'=128,'rep'=4] {'rows'}, use_global_device_ids=true, to_apply=%region_6.7.clone | all-reduce | flops 1024 | bytes 8192
  980.3 0.1 dynamic-slice.2
  980.4 527.6 %reduce-scatter.2.cloned.1.call-done = f32[8,512]{1,0:T(8,128)} async-done(((f32[1024,512]{1,0:T(8,128)}), f32[8,512]{1,0:T(8,128)}) %reduce-scatter.2.cloned.1.call-update) | async-done | bytes 16400 | tf_op jit(solution)/shard_map/reduce_scatter | solution.py:54
  1508.0 136.7 %all-reduce.2 = (f32[8,512]{1,0:T(8,128)}, f32[8]{0:T(128)}) all-reduce(f32[8,512]{1,0:T(8,128)} %reduce-scatter.2.cloned.1.call-done, f32[8]{0:T(128)S(1)} %dynamic-slice.2), channel_id=1, replica_groups=mesh['rows'=128,'rep'=4] {'rep'}, use_global_device_ids=true, to_apply=%region_3.4 | all-reduce | flops 4104 | bytes 32832 | tf_op jit(solution)/shard_map/psum | solution.py:57
  (7 shorter events, 0.0 us)
Async XLA Ops:
  7.2 502.5 %copy-start = (bf16[2048,128]{1,0:T(8,128)(2,1)S(1)}, bf16[2048,128]{1,0:T(8,128)(2,1)}, u32[]{:S(2)}) copy-start(bf16[2048,128]{1,0:T(8,128)(2,1)} %param.4) | copy-start | bytes 1572868
  8.6 498.4 %all-to-all-start = ((bf16[128,8,128]{2,1,0:T(8,128)(2,1)}), bf16[128,8,128]{2,1,0:T(8,128)(2,1)S(1)}, u32[]{:S(2)}, u32[]{:S(2)}) async-start(bf16[128,8,128]{2,1,0:T(8,128)(2,1)} %stack.2), calls=%async_computation | async-start | bytes 524288 | tf_op jit(solution)/shard_map/all_to_all | solution.py:15
  29.0 1479.0 %reduce-scatter.2.cloned.1.call-start = ((), (), s32[]{:S(2)}) async-start(), calls=%async_computation.2 | async-start | bytes 2113536 | tf_op jit(solution)/shard_map/reduce_scatter | solution.py:54
Sparse Core Ops, SparseCore 0:
  516.5 991.4 reduce-scatter.1
